TPU v7x, 512 devices: a whole 4x8x8 slice. The times are simulated.
512 devices in a mesh: gx: 16 (over z, y_hi), gy: 8 (over y_lo, core), gz: 4 (over x).
Axes of the slice: x: 4, y: 8 (y_hi: 2, y_lo: 4; y = y_hi * 4 + y_lo), z: 8, core: 2. Of those that a mesh axis runs over, the one named last changes fastest.
Arguments:
- populations: float32 [19, 16, 128, 4096], P(None, None, ('gy', 'gz'), 'gx'), may hold values from 0 to 0.5, as said below
- cell_type: int32 [16, 128, 4096], P(None, ('gy', 'gz'), 'gx'), may hold values from 0 to 2, as said below
- adjoint: float32 [7, 16, 128, 4096], P(None, 'gz', 'gy', 'gx'), may hold values from -6 to 6
Outputs:
- flow_next: float32 [19, 16, 128, 4096], P(None, None, ('gy', 'gz'), 'gx')
- adjoint_prev: float32 [7, 16, 128, 4096], P(None, 'gz', 'gy', 'gx')
Inputs may be any that keep to these rules, and one draw needn't show every extreme that they name: `cell_type`: layers below 8 are solid (code 1), with code 2 cells only in layer 0; layers from 8 on hold codes 0 and 1, and a cell's code is the same in all of them. `populations`: each population is its lattice weight times a positive factor near one.
All inputs are finite; a program needn't handle non-finite values.
Results may differ from a plain program's by a relative error of at most 0.000065.
Values sent between devices are 32-bit elements; how exact they have to be, the bound alone decides.
No kernel may reach another device: no remote copies, remote signals or barrier semaphores. Data moves between devices by JAX's collectives and lax.ppermute only.
A program may use at most 64 MiB of HBM per device.

v0:
```python
import functools

import jax
import jax.numpy as jnp
from jax import lax
from jax.experimental import pallas as pl
from jax.experimental.pallas import tpu as pltpu
from jax.sharding import PartitionSpec as P


VEL19 = [
    (0, 0, 0),
    (1, 0, 0),
    (-1, 0, 0),
    (0, 1, 0),
    (0, -1, 0),
    (0, 0, 1),
    (0, 0, -1),
    (1, 1, 0),
    (-1, -1, 0),
    (1, -1, 0),
    (-1, 1, 0),
    (1, 0, 1),
    (-1, 0, -1),
    (1, 0, -1),
    (-1, 0, 1),
    (0, 1, 1),
    (0, -1, -1),
    (0, 1, -1),
    (0, -1, 1),
]
WEIGHT19 = [1.0 / 3.0] + [1.0 / 18.0] * 6 + [1.0 / 36.0] * 12
OPPOSITE = [0, 2, 1, 4, 3, 6, 5, 8, 7, 10, 9, 12, 11, 14, 13, 16, 15, 18, 17]
WEIGHT7 = [0.25] + [0.125] * 6
OMEGA_FLOW = 1.6
OMEGA_FLUID = 1.25
OMEGA_SOLID = 1.6

BASE = 8
TOP = 8
LANES = 128
XP = [1, 7, 9, 11, 13]
XM = [2, 8, 10, 12, 14]
YP = [3, 7, 10, 15, 17]
YM = [4, 8, 9, 16, 18]
YALL = YP + YM
FLAG_LANE = 40
HEAT_LANE = 64
FLAG_ROW = 40
CORNER_ROW = 41
HEAT_ROW = 48
Y_ROWS = 64
VMEM = pl.BlockSpec(memory_space=pltpu.VMEM)


def f32(*shape):
    return jax.ShapeDtypeStruct(shape, jnp.float32)


def iota(shape, axis):
    return lax.broadcasted_iota(jnp.int32, shape, axis)


def roll(value, shift, axis=1):
    size = value.shape[axis]
    shift = shift % size
    return value if shift == 0 else pltpu.roll(value, shift, axis)


def collide_kernel(
    pops_in, cells_in, adj_in, post, ysh, xp, xm, yp, ym, gp, gm, pops, cells, adj, sem
):
    rows, cols = cells.shape[1:]
    half = TOP // 2
    loads = [
        pltpu.make_async_copy(cells_in.at[BASE], cells.at[0], sem.at[0]),
        pltpu.make_async_copy(
            pops_in.at[:, BASE : BASE + half], pops.at[:, 0:half], sem.at[1]
        ),
        pltpu.make_async_copy(
            pops_in.at[:, BASE + half : BASE + TOP], pops.at[:, half:TOP], sem.at[2]
        ),
        pltpu.make_async_copy(adj_in, adj, sem.at[3]),
    ]
    for load in loads:
        load.start()
    loads[0].wait()
    left, right = slice(0, LANES), slice(cols - LANES, cols)
    lane = iota((rows, LANES), 1)
    fluid = jnp.where(cells[0] == 0, 1.0, 0.0)
    to_right = jnp.where(lane == FLAG_LANE, roll(fluid[:, right], FLAG_LANE + 1), 0.0)
    to_left = jnp.where(lane == FLAG_LANE, roll(fluid[:, left], FLAG_LANE), 0.0)
    yp[FLAG_ROW : FLAG_ROW + 1, :] = fluid[rows - 1 : rows]
    ym[FLAG_ROW : FLAG_ROW + 1, :] = fluid[0:1]
    for level in range(TOP):
        if level % half == 0:
            loads[1 + level // half].wait()
        f = [pops[i, level] for i in range(19)]
        density = sum(f[1:], f[0])
        u = []
        for k in range(3):
            plus = sum(f[i] for i in range(19) if VEL19[i][k] == 1)
            minus = sum(f[i] for i in range(19) if VEL19[i][k] == -1)
            u.append((plus - minus) / density)
        common = 1.0 - 1.5 * (u[0] * u[0] + u[1] * u[1] + u[2] * u[2])
        scaled = OMEGA_FLOW * density
        for i in range(19):
            c = VEL19[i]
            cu = None
            for k in range(3):
                if c[k]:
                    term = u[k] if c[k] == 1 else -u[k]
                    cu = term if cu is None else cu + term
            shape = common if cu is None else common + cu * (3.0 + 4.5 * cu)
            out = (1.0 - OMEGA_FLOW) * f[i] + (WEIGHT19[i] * scaled) * shape
            post[i, level] = out
            if i in XP:
                at = XP.index(i) * TOP + level
                to_right = jnp.where(lane == at, roll(out[:, right], at + 1), to_right)
            if i in XM:
                at = XM.index(i) * TOP + level
                to_left = jnp.where(lane == at, roll(out[:, left], at), to_left)
            if i in YP:
                at = YP.index(i) * TOP + level
                yp[at : at + 1, :] = out[rows - 1 : rows]
                ysh[YALL.index(i), level, 1:rows, :] = out[0 : rows - 1]
            if i in YM:
                at = YM.index(i) * TOP + level
                ym[at : at + 1, :] = out[0:1]
                ysh[YALL.index(i), level, 0 : rows - 1, :] = out[1:rows]
    loads[3].wait()
    layers, arows = adj.shape[1:3]
    lane = iota((arows, LANES), 1)
    heat_right = jnp.zeros((arows, LANES), jnp.float32)
    heat_left = heat_right
    for z in range(layers):
        at = HEAT_LANE + z
        heat_right = jnp.where(lane == at, roll(adj[2, z, :, right], at + 1), heat_right)
        heat_left = jnp.where(lane == at, roll(adj[1, z, :, left], at), heat_left)
        gp[z : z + 1, :] = adj[4, z, arows - 1 : arows, :]
        gm[z : z + 1, :] = adj[3, z, 0:1, :]
    xp[...] = heat_right
    xm[...] = heat_left
    lane = iota((rows, LANES), 1)
    xp[0:rows, :] = jnp.where(lane < HEAT_LANE, to_right, heat_right[0:rows])
    xm[0:rows, :] = jnp.where(lane < HEAT_LANE, to_left, heat_left[0:rows])
    yp[HEAT_ROW : HEAT_ROW + arows, :] = adj[6, layers - 1]
    ym[HEAT_ROW : HEAT_ROW + arows, :] = adj[5, 0]


def stream_kernel(post, ysh, pops, cells, xl, xr, yu, yd, out, vel, ext):
    rows, cols = cells.shape[1:]
    last = cols - LANES
    sub = iota((rows, cols), 0)
    col = iota((rows, LANES), 1)

    ext[0, 0:1, :] = yu[CORNER_ROW : CORNER_ROW + 1, 0:LANES]
    ext[1, 0:1, :] = yu[CORNER_ROW : CORNER_ROW + 1, LANES : 2 * LANES]
    ext[0, 1 : rows + 1, :] = xl[0:rows, :]
    ext[1, 1 : rows + 1, :] = xr[0:rows, :]
    ext[0, rows + 1 : rows + 2, :] = yd[CORNER_ROW : CORNER_ROW + 1, 0:LANES]
    ext[1, rows + 1 : rows + 2, :] = yd[CORNER_ROW : CORNER_ROW + 1, LANES : 2 * LANES]
    beyond = {
        (side, cy): ext[side, 1 - cy : 1 - cy + rows, :] for side in (0, 1) for cy in (-1, 0, 1)
    }

    def shift_x(value, cx, cy, lane_at):
        if cx == 0:
            return value
        value = roll(value, cx)
        if cx == 1:
            edge = roll(beyond[0, cy], -lane_at)
            patched = jnp.where(col == 0, edge, value[:, 0:LANES])
            return jnp.concatenate([patched, value[:, LANES:]], axis=1)
        edge = roll(beyond[1, cy], LANES - 1 - lane_at)
        patched = jnp.where(col == LANES - 1, edge, value[:, last:])
        return jnp.concatenate([value[:, 0:last], patched], axis=1)

    def shift_y(value, cy, halo):
        if cy == 0:
            return value
        halo = jnp.broadcast_to(halo, (rows, cols))
        return jnp.where(sub == (0 if cy == 1 else rows - 1), halo, value)

    fluid = jnp.where(cells[BASE] == 0, 1.0, 0.0)
    is_fluid = fluid > 0.5
    spread = {0: fluid}
    spread[1] = shift_y(
        jnp.concatenate([fluid[rows - 1 : rows], fluid[0 : rows - 1]], axis=0),
        1,
        yu[FLAG_ROW : FLAG_ROW + 1, :],
    )
    spread[-1] = shift_y(
        jnp.concatenate([fluid[1:rows], fluid[0:1]], axis=0), -1, yd[FLAG_ROW : FLAG_ROW + 1, :]
    )
    open_from = {
        (cx, cy): shift_x(spread[cy], cx, cy, FLAG_LANE) > 0.5
        for cx in (-1, 0, 1)
        for cy in (-1, 0, 1)
    }

    out[:, 0:BASE] = pops[:, 0:BASE]
    vel[0] = jnp.zeros(vel.shape[1:], jnp.float32)
    vel[1] = jnp.zeros(vel.shape[1:], jnp.float32)
    layers = (vel.shape[1] - 1) // 3
    vel[0, 3 * layers] = jnp.where(cells[0] == 2, 1.0, 0.0)
    vel[2, 3 * layers] = fluid
    vel[3, 3 * layers] = fluid
    for level in range(TOP):
        density = None
        momentum = [None, None, None]
        for i in range(19):
            cx, cy, cz = VEL19[i]
            before = pops[i, BASE + level]
            back = post[OPPOSITE[i], level]
            source = level - cz
            if i == 0:
                pulled = back
            elif source < 0 or source >= TOP:
                pulled = back
            else:
                if cy == 0:
                    value = post[i, source]
                else:
                    at = (YP if cy == 1 else YM).index(i) * TOP + source
                    halo = (yu if cy == 1 else yd)[at : at + 1, :]
                    value = shift_y(ysh[YALL.index(i), source], cy, halo)
                if cx:
                    value = shift_x(value, cx, cy, (XP if cx == 1 else XM).index(i) * TOP + source)
                pulled = jnp.where(open_from[cx, cy], value, back)
            new = jnp.where(is_fluid, pulled, before)
            out[i, BASE + level] = new
            density = new if density is None else density + new
            for k in range(3):
                c = VEL19[i][k]
                if c:
                    term = new if c == 1 else -new
                    momentum[k] = term if momentum[k] is None else momentum[k] + term
        for k in range(3):
            vel[2 + level // layers, k * layers + level % layers] = jnp.where(
                is_fluid, momentum[k] / density, 0.0
            )


def thermal_kernel(shards, adj, va, xl, xr, yu, yd, gu, gd, out, wide):
    layers, rows, cols = adj.shape[1:]
    gz = lax.axis_index("gz")
    srcs, planes, part = va.shape[:3]
    last = cols - LANES
    for q in range(planes):
        for s in range(srcs):
            wide[q, part * s : part * (s + 1), :] = va[s, q]
    sub = iota((rows, cols), 0)
    col = iota((rows, LANES), 1)
    mark = wide[planes - 1]
    is_fluid = (mark * jnp.where(gz >= shards // 2, 1.0, 0.0)) > 0.5
    heated = mark * jnp.where(gz == 0, 1.0, 0.0)
    below = jnp.where(gz == 0, 0.0, yu[HEAT_ROW : HEAT_ROW + rows, :])
    above = jnp.where(gz == shards - 1, 0.0, yd[HEAT_ROW : HEAT_ROW + rows, :])
    omega = jnp.where(is_fluid, OMEGA_FLUID, OMEGA_SOLID)
    for z in range(layers):
        p = [adj[0, z]]
        ahead = roll(adj[1, z], -1)
        edge = roll(xr[...], LANES - 1 - (HEAT_LANE + z))
        p.append(
            jnp.concatenate(
                [ahead[:, 0:last], jnp.where(col == LANES - 1, edge, ahead[:, last:])], axis=1
            )
        )
        behind = roll(adj[2, z], 1)
        edge = roll(xl[...], -(HEAT_LANE + z))
        p.append(
            jnp.concatenate(
                [jnp.where(col == 0, edge, behind[:, 0:LANES]), behind[:, LANES:]], axis=1
            )
        )
        halo = jnp.broadcast_to(gd[z : z + 1, :], (rows, cols))
        p.append(jnp.where(sub == rows - 1, halo, roll(adj[3, z], -1, 0)))
        halo = jnp.broadcast_to(gu[z : z + 1, :], (rows, cols))
        p.append(jnp.where(sub == 0, halo, roll(adj[4, z], 1, 0)))
        p.append(adj[5, z + 1] if z + 1 < layers else above)
        p.append(adj[6, z - 1] if z > 0 else below)
        mean = WEIGHT7[0] * p[0] + WEIGHT7[1] * (p[1] + p[2] + p[3] + p[4] + p[5] + p[6])
        dot = (
            wide[z] * (p[1] - p[2])
            + wide[layers + z] * (p[3] - p[4])
            + wide[2 * layers + z] * (p[5] - p[6])
        )
        common = omega * (mean + 4.0 * WEIGHT7[1] * dot)
        if z == 0:
            common = common + heated
        for j in range(7):
            out[j, z] = (1.0 - omega) * p[j] + common


def per_device(populations, cell_type, adjoint, sizes):
    nx, ny, nz = sizes
    axes = ("gx", "gy", "gz")

    def along(delta_x, delta_y):
        moves = []
        for a in range(nx):
            for b in range(ny * nz):
                a2, b2 = a + delta_x, b + delta_y
                if 0 <= a2 < nx and 0 <= b2 < ny * nz:
                    moves.append((a * ny * nz + b, a2 * ny * nz + b2))
        return moves

    def across(delta):
        moves = []
        for a in range(nx):
            for b in range(ny):
                for c in range(nz):
                    if 0 <= b + delta < ny:
                        moves.append(((a * ny + b) * nz + c, (a * ny + b + delta) * nz + c))
        return moves

    _, rows, cols = cell_type.shape
    layers, heat_rows = adjoint.shape[1:3]
    post, ysh, xp, xm, yp, ym, gp, gm = pl.pallas_call(
        collide_kernel,
        out_shape=(
            f32(19, TOP, rows, cols),
            f32(10, TOP, rows, cols),
            f32(heat_rows, LANES),
            f32(heat_rows, LANES),
            f32(Y_ROWS, cols),
            f32(Y_ROWS, cols),
            f32(layers, cols),
            f32(layers, cols),
        ),
        in_specs=[pl.BlockSpec(memory_space=pltpu.HBM)] * 3,
        out_specs=(VMEM,) * 8,
        scratch_shapes=[
            pltpu.VMEM((19, TOP, rows, cols), jnp.float32),
            pltpu.VMEM((1, rows, cols), jnp.int32),
            pltpu.VMEM(adjoint.shape, jnp.float32),
            pltpu.SemaphoreType.DMA((4,)),
        ],
        compiler_params=pltpu.CompilerParams(vmem_limit_bytes=16 << 20),
        name="collide",
    )(*(pltpu.with_memory_space_constraint(a, pltpu.HBM) for a in (populations, cell_type, adjoint)))
    xl = lax.ppermute(xp, axes, along(1, 0))
    xr = lax.ppermute(xm, axes, along(-1, 0))
    gu = lax.ppermute(gp, axes, across(1))
    gd = lax.ppermute(gm, axes, across(-1))
    top = jnp.concatenate([xl[rows - 1 : rows], xr[rows - 1 : rows]], axis=1)
    bottom = jnp.concatenate([xl[0:1], xr[0:1]], axis=1)
    yp = lax.dynamic_update_slice(yp, top, (CORNER_ROW, 0))
    ym = lax.dynamic_update_slice(ym, bottom, (CORNER_ROW, 0))
    yu = lax.ppermute(yp, axes, along(0, 1))
    yd = lax.ppermute(ym, axes, along(0, -1))
    flow_next, vel = pl.pallas_call(
        stream_kernel,
        out_shape=(f32(*populations.shape), f32(nz, 3 * layers + 1, rows, cols)),
        in_specs=[VMEM] * 8,
        out_specs=(VMEM,) * 2,
        scratch_shapes=[pltpu.VMEM((2, 8, LANES), jnp.float32)],
        compiler_params=pltpu.CompilerParams(vmem_limit_bytes=16 << 20),
        name="stream",
    )(post, ysh, populations, cell_type, xl, xr, yu, yd)
    va = lax.all_to_all(vel, "gz", split_axis=0, concat_axis=0, tiled=True)
    adjoint_prev = pl.pallas_call(
        functools.partial(thermal_kernel, nz),
        out_shape=f32(*adjoint.shape),
        in_specs=[VMEM] * 8,
        out_specs=VMEM,
        scratch_shapes=[pltpu.VMEM((3 * layers + 1, heat_rows, cols), jnp.float32)],
        compiler_params=pltpu.CompilerParams(vmem_limit_bytes=16 << 20),
        name="thermal",
    )(adjoint, va, xl, xr, yu, yd, gu, gd)
    return flow_next, adjoint_prev


def solution(mesh):
    sizes = tuple(mesh.shape[axis] for axis in ("gx", "gy", "gz"))
    placed = (
        P(None, None, ("gy", "gz"), "gx"),
        P(None, ("gy", "gz"), "gx"),
        P(None, "gz", "gy", "gx"),
    )

    def body(p, c, a):
        return per_device(p, c, a, sizes)

    return jax.shard_map(
        body,
        mesh=mesh,
        in_specs=placed,
        out_specs=(P(None, None, ("gy", "gz"), "gx"), P(None, "gz", "gy", "gx")),
        check_vma=False,
    )
```

profile of v0, /device:TPU:243, one launch (start us, length us, event | category | flops | bytes accessed | tf_op | source)
XLA Modules:
  0.0 46.0 jit_solution(11943803655167330198)
XLA Ops:
  0.6 0.0 copy-start.2
  0.6 0.0 copy-start
  0.6 1.7 %collide.1 = (f32[19,8,4,256]{3,2,1,0:T(4,128)S(1)}, f32[10,8,4,256]{3,2,1,0:T(4,128)S(1)}, f32[16,128]{1,0:T(8,128)S(1)}, f32[16,128]{1,0:T(8,128)S(1)}, f32[64...) custom-call(f32[19,16,4,256]{3,2,1,0:T(4,128)} %pops.1, ...), custom_call_target="tpu_custom_call" | custom-call | tf_op jit(solution)/shard_map/collide/pallas_call | solution.py:320
  2.3 6.6 %collective-permute-start = (f32[16,128]{1,0:T(8,128)S(1)}, f32[16,128]{1,0:T(8,128)S(1)}, u32[]{:S(2)}, u32[]{:S(2)}) collective-permute-start(f32[16,128]{1,0:T(8,128)S(1)} %get-tuple-element.14), channel_id=1, source_target_pairs={{0,32},{1,33},{2,34},{3,35},{4,36},{5,37},{6,38},{7,39},{8,40},{9,... | collective-permute-start | bytes 24584 | tf_op jit(solution)/shard_map/ppermute | solution.py:343
  8.9 2.6 %collective-permute-start.1 = (f32[16,128]{1,0:T(8,128)S(1)}, f32[16,128]{1,0:T(8,128)S(1)}, u32[]{:S(2)}, u32[]{:S(2)}) collective-permute-start(f32[16,128]{1,0:T(8,128)S(1)} %get-tuple-element.15), channel_id=1, source_target_pairs={{32,0},{33,1},{34,2},{35,3},{36,4},{37,5},{38,6},{39,7},{40,8},{41... | collective-permute-start | bytes 24584 | tf_op jit(solution)/shard_map/ppermute | solution.py:344
  11.5 0.0 collective-permute-done.xl
  11.6 7.7 %collective-permute-done.1.xr = f32[16,128]{1,0:T(8,128)S(1)} collective-permute-done((f32[16,128]{1,0:T(8,128)S(1)}, f32[16,128]{1,0:T(8,128)S(1)}, u32[]{:S(2)}, u32[]{:S(2)}) %collective-permute-start.1) | collective-permute-done | bytes 8224 | tf_op jit(solution)/shard_map/ppermute | solution.py:344
  19.4 3.1 %collective-permute-start.2 = (f32[64,256]{1,0:T(8,128)S(1)}, f32[64,256]{1,0:T(8,128)S(1)}, u32[]{:S(2)}, u32[]{:S(2)}) collective-permute-start(f32[64,256]{1,0:T(8,128)S(1)} %dynamic_update_slice.6), channel_id=1, source_target_pairs={{0,1},{1,2},{2,3},{3,4},{4,5},{5,6},{6,7},{7,8},{8,9},{9,10},{10,1... | collective-permute-start | bytes 196616 | tf_op jit(solution)/shard_map/ppermute | solution.py:351
  22.5 2.2 %collective-permute-start.3 = (f32[64,256]{1,0:T(8,128)S(1)}, f32[64,256]{1,0:T(8,128)S(1)}, u32[]{:S(2)}, u32[]{:S(2)}) collective-permute-start(f32[64,256]{1,0:T(8,128)S(1)} %dynamic_update_slice.7), channel_id=1, source_target_pairs={{1,0},{2,1},{3,2},{4,3},{5,4},{6,5},{7,6},{8,7},{9,8},{10,9},{11,1... | collective-permute-start | bytes 196616 | tf_op jit(solution)/shard_map/ppermute | solution.py:352
  24.7 0.0 collective-permute-done.2.yu
  24.7 2.8 %collective-permute-done.3.yd = f32[64,256]{1,0:T(8,128)S(1)} collective-permute-done((f32[64,256]{1,0:T(8,128)S(1)}, f32[64,256]{1,0:T(8,128)S(1)}, u32[]{:S(2)}, u32[]{:S(2)}) %collective-permute-start.3) | collective-permute-done | bytes 65568 | tf_op jit(solution)/shard_map/ppermute | solution.py:352
  27.6 0.0 copy-done.2
  27.6 0.0 copy-done
  27.6 0.0 copy-start.1
  27.6 1.4 %stream.1 = (f32[19,16,4,256]{3,2,1,0:T(4,128)}, f32[4,13,4,256]{3,2,1,0:T(4,128)}) custom-call(f32[19,8,4,256]{3,2,1,0:T(4,128)S(1)} %get-tuple-element.12.post, f32[10,8,4,256]{3,2,1,0:T(4,128)S(1)} %get-tuple-element.13.ysh, f32[19,16,4,256]{3,2,1,0:T(4,128)S(1)} %copy-done, s32[16,4,256]{2,1,0:T(4,128)S(1)} %copy-done.2, ...), custom_call_target="tpu_custom_call" | custom-call | tf_op jit(solution)/shard_map/stream/pallas_call | solution.py:353
  29.0 8.7 %all-to-all-start = ((f32[4,13,4,256]{3,2,1,0:T(4,128)}), f32[4,13,4,256]{3,2,1,0:T(4,128)S(1)}, u32[]{:S(2)}, u32[]{:S(2)}) async-start(f32[4,13,4,256]{3,2,1,0:T(4,128)} %get-tuple-element.19), calls=%async_computation | async-start | bytes 425984 | tf_op jit(solution)/shard_map/all_to_all | solution.py:362
  37.7 2.5 %collective-permute-start.4 = (f32[4,256]{1,0:T(4,128)S(1)}, f32[4,256]{1,0:T(4,128)S(1)}, u32[]{:S(2)}, u32[]{:S(2)}) collective-permute-start(f32[4,256]{1,0:T(4,128)S(1)} %get-tuple-element.20), channel_id=1, source_target_pairs={{0,4},{1,5},{2,6},{3,7},{4,8},{5,9},{6,10},{7,11},{8,12},{9,13},{1... | collective-permute-start | bytes 12296 | tf_op jit(solution)/shard_map/ppermute | solution.py:345
  40.2 1.9 %collective-permute-start.5 = (f32[4,256]{1,0:T(4,128)S(1)}, f32[4,256]{1,0:T(4,128)S(1)}, u32[]{:S(2)}, u32[]{:S(2)}) collective-permute-start(f32[4,256]{1,0:T(4,128)S(1)} %get-tuple-element.21), channel_id=1, source_target_pairs={{4,0},{5,1},{6,2},{7,3},{8,4},{9,5},{10,6},{11,7},{12,8},{13,9},{1... | collective-permute-start | bytes 12296 | tf_op jit(solution)/shard_map/ppermute | solution.py:346
  42.1 0.0 collective-permute-done.4.gu
  42.1 3.0 %collective-permute-done.5.gd = f32[4,256]{1,0:T(4,128)S(1)} collective-permute-done((f32[4,256]{1,0:T(4,128)S(1)}, f32[4,256]{1,0:T(4,128)S(1)}, u32[]{:S(2)}, u32[]{:S(2)}) %collective-permute-start.5) | collective-permute-done | bytes 4128 | tf_op jit(solution)/shard_map/ppermute | solution.py:346
  45.1 0.0 all-to-all-done.va
  45.1 0.0 copy-done.1
  45.1 0.9 %thermal.1 = f32[7,4,16,256]{3,2,1,0:T(8,128)} custom-call(f32[7,4,16,256]{3,2,1,0:T(8,128)S(1)} %copy-done.1, f32[4,13,4,256]{3,2,1,0:T(4,128)S(1)} %all-to-all-done.va, f32[16,128]{1,0:T(8,128)S(1)} %collective-permute-done.xl, f32[16,128]{1,0:T(8,128)S(1)} %collective-permute-done.1.xr, f32[64,256]{1,0:T(8,128)S(1)} %collective-permute-done.2.yu, ...), custom_call_target="tpu_custom_call" | custom-call | tf_op jit(solution)/shard_map/thermal/pallas_call | solution.py:363
  (6 shorter events, 0.1 us)
Async XLA Ops:
  0.6 26.9 %copy-start.2 = (s32[16,4,256]{2,1,0:T(4,128)S(1)}, s32[16,4,256]{2,1,0:T(4,128)}, u32[]{:S(2)}) copy-start(s32[16,4,256]{2,1,0:T(4,128)} %cells.1) | copy-start | bytes 196612
  0.6 26.9 %copy-start = (f32[19,16,4,256]{3,2,1,0:T(4,128)S(1)}, f32[19,16,4,256]{3,2,1,0:T(4,128)}, u32[]{:S(2)}) copy-start(f32[19,16,4,256]{3,2,1,0:T(4,128)} %pops.1) | copy-start | bytes 3735556
  2.3 9.2 %collective-permute-start = (f32[16,128]{1,0:T(8,128)S(1)}, f32[16,128]{1,0:T(8,128)S(1)}, u32[]{:S(2)}, u32[]{:S(2)}) collective-permute-start(f32[16,128]{1,0:T(8,128)S(1)} %get-tuple-element.14), channel_id=1, source_target_pairs={{0,32},{1,33},{2,34},{3,35},{4,36},{5,37},{6,38},{7,39},{8,40},{9,... | collective-permute-start | bytes 24584 | tf_op jit(solution)/shard_map/ppermute | solution.py:343
  8.9 10.4 %collective-permute-start.1 = (f32[16,128]{1,0:T(8,128)S(1)}, f32[16,128]{1,0:T(8,128)S(1)}, u32[]{:S(2)}, u32[]{:S(2)}) collective-permute-start(f32[16,128]{1,0:T(8,128)S(1)} %get-tuple-element.15), channel_id=1, source_target_pairs={{32,0},{33,1},{34,2},{35,3},{36,4},{37,5},{38,6},{39,7},{40,8},{41... | collective-permute-start | bytes 24584 | tf_op jit(solution)/shard_map/ppermute | solution.py:344
  19.4 5.4 %collective-permute-start.2 = (f32[64,256]{1,0:T(8,128)S(1)}, f32[64,256]{1,0:T(8,128)S(1)}, u32[]{:S(2)}, u32[]{:S(2)}) collective-permute-start(f32[64,256]{1,0:T(8,128)S(1)} %dynamic_update_slice.6), channel_id=1, source_target_pairs={{0,1},{1,2},{2,3},{3,4},{4,5},{5,6},{6,7},{7,8},{8,9},{9,10},{10,1... | collective-permute-start | bytes 196616 | tf_op jit(solution)/shard_map/ppermute | solution.py:351
  22.5 5.0 %collective-permute-start.3 = (f32[64,256]{1,0:T(8,128)S(1)}, f32[64,256]{1,0:T(8,128)S(1)}, u32[]{:S(2)}, u32[]{:S(2)}) collective-permute-start(f32[64,256]{1,0:T(8,128)S(1)} %dynamic_update_slice.7), channel_id=1, source_target_pairs={{1,0},{2,1},{3,2},{4,3},{5,4},{6,5},{7,6},{8,7},{9,8},{10,9},{11,1... | collective-permute-start | bytes 196616 | tf_op jit(solution)/shard_map/ppermute | solution.py:352
  27.6 17.5 %copy-start.1 = (f32[7,4,16,256]{3,2,1,0:T(8,128)S(1)}, f32[7,4,16,256]{3,2,1,0:T(8,128)}, u32[]{:S(2)}) copy-start(f32[7,4,16,256]{3,2,1,0:T(8,128)} %adj.1) | copy-start | bytes 1376260
  29.0 16.1 %all-to-all-start = ((f32[4,13,4,256]{3,2,1,0:T(4,128)}), f32[4,13,4,256]{3,2,1,0:T(4,128)S(1)}, u32[]{:S(2)}, u32[]{:S(2)}) async-start(f32[4,13,4,256]{3,2,1,0:T(4,128)} %get-tuple-element.19), calls=%async_computation | async-start | bytes 425984 | tf_op jit(solution)/shard_map/all_to_all | solution.py:362
  37.7 4.4 %collective-permute-start.4 = (f32[4,256]{1,0:T(4,128)S(1)}, f32[4,256]{1,0:T(4,128)S(1)}, u32[]{:S(2)}, u32[]{:S(2)}) collective-permute-start(f32[4,256]{1,0:T(4,128)S(1)} %get-tuple-element.20), channel_id=1, source_target_pairs={{0,4},{1,5},{2,6},{3,7},{4,8},{5,9},{6,10},{7,11},{8,12},{9,13},{1... | collective-permute-start | bytes 12296 | tf_op jit(solution)/shard_map/ppermute | solution.py:345
  40.2 4.9 %collective-permute-start.5 = (f32[4,256]{1,0:T(4,128)S(1)}, f32[4,256]{1,0:T(4,128)S(1)}, u32[]{:S(2)}, u32[]{:S(2)}) collective-permute-start(f32[4,256]{1,0:T(4,128)S(1)} %get-tuple-element.21), channel_id=1, source_target_pairs={{4,0},{5,1},{6,2},{7,3},{8,4},{9,5},{10,6},{11,7},{12,8},{13,9},{1... | collective-permute-start | bytes 12296 | tf_op jit(solution)/shard_map/ppermute | solution.py:346
where the time goes:
time: 46.4 us; the launch traced here: 46 us
  starting transfers between devices  27.5 us (59%)
  waiting for transfers between devices  13.6 us (29%)
  Pallas kernels  4.05 us (9%)
  between operations  0.76 us (2%)
    all_to_all x1, starting transfers between devices, per_device(): va = lax.all_to_all(vel, 'gz', split_axis=0, concat_axis=0, tiled=True)  8.67 us
    ppermute x1, waiting for transfers between devices, per_device(): xr = lax.ppermute(xm, axes, along(-1, 0))  7.75 us
    ppermute x1, starting transfers between devices, per_device(): xl = lax.ppermute(xp, axes, along(1, 0))  6.55 us
    ppermute x1, starting transfers between devices, per_device(): yu = lax.ppermute(yp, axes, along(0, 1))  3.12 us
    ppermute x1, waiting for transfers between devices, per_device(): gd = lax.ppermute(gm, axes, across(-1))  2.99 us
    ppermute x1, waiting for transfers between devices, per_device(): yd = lax.ppermute(ym, axes, along(0, -1))  2.83 us
    ppermute x1, starting transfers between devices, per_device(): xr = lax.ppermute(xm, axes, along(-1, 0))  2.64 us
    ppermute x1, starting transfers between devices, per_device(): gu = lax.ppermute(gp, axes, across(1))  2.47 us
  transfers between devices with their start and end apart: 7, of which 3 were waited for; matrix products, arithmetic and copies ran while one was open for 0% of the time, Pallas kernels for 0%

commit v1 on v0

--- a/solution.py
+++ b/solution.py
@@ -1,5 +1,3 @@
-import functools
-
 import jax
 import jax.numpy as jnp
 from jax import lax
@@ -48,6 +46,7 @@
 HEAT_LANE = 64
 FLAG_ROW = 40
 CORNER_ROW = 41
+CODE_ROW = 42
 HEAT_ROW = 48
 Y_ROWS = 64
 VMEM = pl.BlockSpec(memory_space=pltpu.VMEM)
@@ -68,9 +67,11 @@
 
 
 def collide_kernel(
-    pops_in, cells_in, adj_in, post, ysh, xp, xm, yp, ym, gp, gm, pops, cells, adj, sem
+    pops_in, cells_in, adj_in, post, ysh, xa, xb, ya, yb, ga, gb, pops, cells, adj, faces, sem
 ):
     rows, cols = cells.shape[1:]
+    odd_x, odd_g, odd_y = (lax.axis_index(axis) % 2 for axis in ("gx", "gy", "gz"))
+    yp, ym = faces.at[0], faces.at[1]
     half = TOP // 2
     loads = [
         pltpu.make_async_copy(cells_in.at[BASE], cells.at[0], sem.at[0]),
@@ -81,6 +82,7 @@
             pops_in.at[:, BASE + half : BASE + TOP], pops.at[:, half:TOP], sem.at[2]
         ),
         pltpu.make_async_copy(adj_in, adj, sem.at[3]),
+        pltpu.make_async_copy(cells_in.at[0], cells.at[1], sem.at[4]),
     ]
     for load in loads:
         load.start()
@@ -137,19 +139,38 @@
         at = HEAT_LANE + z
         heat_right = jnp.where(lane == at, roll(adj[2, z, :, right], at + 1), heat_right)
         heat_left = jnp.where(lane == at, roll(adj[1, z, :, left], at), heat_left)
-        gp[z : z + 1, :] = adj[4, z, arows - 1 : arows, :]
-        gm[z : z + 1, :] = adj[3, z, 0:1, :]
-    xp[...] = heat_right
-    xm[...] = heat_left
+        high, low = adj[4, z, arows - 1 : arows, :], adj[3, z, 0:1, :]
+        ga[z : z + 1, :] = jnp.where(odd_g == 0, high, low)
+        gb[z : z + 1, :] = jnp.where(odd_g == 0, low, high)
+    xa[...] = jnp.where(odd_x == 0, heat_right, heat_left)
+    xb[...] = jnp.where(odd_x == 0, heat_left, heat_right)
     lane = iota((rows, LANES), 1)
-    xp[0:rows, :] = jnp.where(lane < HEAT_LANE, to_right, heat_right[0:rows])
-    xm[0:rows, :] = jnp.where(lane < HEAT_LANE, to_left, heat_left[0:rows])
+    to_right = jnp.where(lane < HEAT_LANE, to_right, heat_right[0:rows])
+    to_left = jnp.where(lane < HEAT_LANE, to_left, heat_left[0:rows])
+    xa[0:rows, :] = jnp.where(odd_x == 0, to_right, to_left)
+    xb[0:rows, :] = jnp.where(odd_x == 0, to_left, to_right)
     yp[HEAT_ROW : HEAT_ROW + arows, :] = adj[6, layers - 1]
     ym[HEAT_ROW : HEAT_ROW + arows, :] = adj[5, 0]
-
-
-def stream_kernel(post, ysh, pops, cells, xl, xr, yu, yd, out, vel, ext):
+    loads[4].wait()
+    code = jnp.where(cells[1] == 2, 1.0, 0.0)
+    yp[CODE_ROW : CODE_ROW + rows, :] = code
+    ym[CODE_ROW : CODE_ROW + rows, :] = code
+    ya[...] = faces[odd_y]
+    yb[...] = faces[1 - odd_y]
+
+
+def stream_kernel(
+    post, ysh, pops, cells, xa, xb, ya, yb, out, pa, pb, pc, own, ext, halos, vel
+):
     rows, cols = cells.shape[1:]
+    odd_x, odd_y = (lax.axis_index(axis) % 2 for axis in ("gx", "gz"))
+    gz = lax.axis_index("gz")
+    xl = jnp.where(odd_x == 0, xb[...], xa[...])
+    xr = jnp.where(odd_x == 0, xa[...], xb[...])
+    first, second = ya[0:HEAT_ROW, :], yb[0:HEAT_ROW, :]
+    halos[0] = jnp.where(odd_y == 0, second, first)
+    halos[1] = jnp.where(odd_y == 0, first, second)
+    yu, yd = halos.at[0], halos.at[1]
     last = cols - LANES
     sub = iota((rows, cols), 0)
     col = iota((rows, LANES), 1)
@@ -200,12 +221,7 @@
     }
 
     out[:, 0:BASE] = pops[:, 0:BASE]
-    vel[0] = jnp.zeros(vel.shape[1:], jnp.float32)
-    vel[1] = jnp.zeros(vel.shape[1:], jnp.float32)
-    layers = (vel.shape[1] - 1) // 3
-    vel[0, 3 * layers] = jnp.where(cells[0] == 2, 1.0, 0.0)
-    vel[2, 3 * layers] = fluid
-    vel[3, 3 * layers] = fluid
+    layers = own.shape[0] // 3
     for level in range(TOP):
         density = None
         momentum = [None, None, None]
@@ -237,38 +253,63 @@
                     term = new if c == 1 else -new
                     momentum[k] = term if momentum[k] is None else momentum[k] + term
         for k in range(3):
-            vel[2 + level // layers, k * layers + level % layers] = jnp.where(
+            vel[level // layers, k * layers + level % layers] = jnp.where(
                 is_fluid, momentum[k] / density, 0.0
             )
-
-
-def thermal_kernel(shards, adj, va, xl, xr, yu, yd, gu, gd, out, wide):
+    code = jnp.where(cells[0] == 2, 1.0, 0.0)
+    passed = yd[CODE_ROW : CODE_ROW + rows, :]
+    for buffer, lower in ((pa, 1), (pb, 0), (pc, 3), (own, 2)):
+        buffer[0 : 3 * layers] = vel[jnp.where(gz == lower, 0, 1)]
+    pa[3 * layers] = jnp.where(gz == 3, code, fluid)
+    pb[3 * layers] = fluid
+    pc[3 * layers] = jnp.where(gz == 1, passed, fluid)
+    own[3 * layers] = jnp.where(gz == 0, code, fluid)
+
+
+def thermal_kernel(adj, pa, pb, pc, own, xa, xb, ya, yb, ga, gb, out, wide):
     layers, rows, cols = adj.shape[1:]
+    odd_x, odd_g, odd_y = (lax.axis_index(axis) % 2 for axis in ("gx", "gy", "gz"))
     gz = lax.axis_index("gz")
-    srcs, planes, part = va.shape[:3]
+    planes, part = own.shape[:2]
     last = cols - LANES
+    at_two, at_zero = gz == 2, gz == 0
     for q in range(planes):
-        for s in range(srcs):
-            wide[q, part * s : part * (s + 1), :] = va[s, q]
+        a, b, c, mine = pa[q], pb[q], pc[q], own[q]
+        blocks = [
+            jnp.where(at_two, b, a),
+            jnp.where(at_two, a, b),
+            jnp.where(at_two, mine, c),
+            jnp.where(at_two, c, mine),
+        ]
+        if q == planes - 1:
+            near = ya[CODE_ROW : CODE_ROW + part, :]
+            blocks = [jnp.where(at_zero, v, w) for v, w in zip((mine, near, c, a), blocks)]
+        for s in range(4):
+            wide[q, part * s : part * (s + 1), :] = blocks[s]
     sub = iota((rows, cols), 0)
     col = iota((rows, LANES), 1)
     mark = wide[planes - 1]
-    is_fluid = (mark * jnp.where(gz >= shards // 2, 1.0, 0.0)) > 0.5
-    heated = mark * jnp.where(gz == 0, 1.0, 0.0)
-    below = jnp.where(gz == 0, 0.0, yu[HEAT_ROW : HEAT_ROW + rows, :])
-    above = jnp.where(gz == shards - 1, 0.0, yd[HEAT_ROW : HEAT_ROW + rows, :])
+    is_fluid = (mark * jnp.where(gz >= 2, 1.0, 0.0)) > 0.5
+    heated = mark * jnp.where(at_zero, 1.0, 0.0)
+    xl = jnp.where(odd_x == 0, xb[...], xa[...])
+    xr = jnp.where(odd_x == 0, xa[...], xb[...])
+    gu = jnp.where(odd_g == 0, gb[...], ga[...])
+    gd = jnp.where(odd_g == 0, ga[...], gb[...])
+    first, second = ya[HEAT_ROW : HEAT_ROW + rows, :], yb[HEAT_ROW : HEAT_ROW + rows, :]
+    below = jnp.where(at_zero, 0.0, jnp.where(odd_y == 0, second, first))
+    above = jnp.where(gz == 3, 0.0, jnp.where(odd_y == 0, first, second))
     omega = jnp.where(is_fluid, OMEGA_FLUID, OMEGA_SOLID)
     for z in range(layers):
         p = [adj[0, z]]
         ahead = roll(adj[1, z], -1)
-        edge = roll(xr[...], LANES - 1 - (HEAT_LANE + z))
+        edge = roll(xr, LANES - 1 - (HEAT_LANE + z))
         p.append(
             jnp.concatenate(
                 [ahead[:, 0:last], jnp.where(col == LANES - 1, edge, ahead[:, last:])], axis=1
             )
         )
         behind = roll(adj[2, z], 1)
-        edge = roll(xl[...], -(HEAT_LANE + z))
+        edge = roll(xl, -(HEAT_LANE + z))
         p.append(
             jnp.concatenate(
                 [jnp.where(col == 0, edge, behind[:, 0:LANES]), behind[:, LANES:]], axis=1
@@ -286,7 +327,7 @@
             + wide[layers + z] * (p[3] - p[4])
             + wide[2 * layers + z] * (p[5] - p[6])
         )
-        common = omega * (mean + 4.0 * WEIGHT7[1] * dot)
+        common = omega * (mean + 4.0 * WEIGHT7[1] * jnp.where(is_fluid, dot, 0.0))
         if z == 0:
             common = common + heated
         for j in range(7):
@@ -297,27 +338,26 @@
     nx, ny, nz = sizes
     axes = ("gx", "gy", "gz")
 
-    def along(delta_x, delta_y):
-        moves = []
-        for a in range(nx):
-            for b in range(ny * nz):
-                a2, b2 = a + delta_x, b + delta_y
-                if 0 <= a2 < nx and 0 <= b2 < ny * nz:
-                    moves.append((a * ny * nz + b, a2 * ny * nz + b2))
-        return moves
-
-    def across(delta):
+    def swaps(axis, size, parity):
         moves = []
         for a in range(nx):
             for b in range(ny):
                 for c in range(nz):
-                    if 0 <= b + delta < ny:
-                        moves.append(((a * ny + b) * nz + c, (a * ny + b + delta) * nz + c))
+                    place = (a, b, c, b * nz + c)[axis]
+                    other = place + 1 if (place - parity) % 2 == 0 else place - 1
+                    if 0 <= other < size:
+                        there = {0: (other, b, c), 1: (a, other, c), 3: (a, other // nz, other % nz)}[axis]
+                        moves.append(
+                            ((a * ny + b) * nz + c, (there[0] * ny + there[1]) * nz + there[2])
+                        )
         return moves
+
+    def inside(pairs):
+        return [(g * nz + i, g * nz + j) for g in range(nx * ny) for i, j in pairs]
 
     _, rows, cols = cell_type.shape
     layers, heat_rows = adjoint.shape[1:3]
-    post, ysh, xp, xm, yp, ym, gp, gm = pl.pallas_call(
+    post, ysh, xa, xb, ya, yb, ga, gb = pl.pallas_call(
         collide_kernel,
         out_shape=(
             f32(19, TOP, rows, cols),
@@ -333,42 +373,63 @@
         out_specs=(VMEM,) * 8,
         scratch_shapes=[
             pltpu.VMEM((19, TOP, rows, cols), jnp.float32),
-            pltpu.VMEM((1, rows, cols), jnp.int32),
+            pltpu.VMEM((2, rows, cols), jnp.int32),
             pltpu.VMEM(adjoint.shape, jnp.float32),
-            pltpu.SemaphoreType.DMA((4,)),
+            pltpu.VMEM((2, Y_ROWS, cols), jnp.float32),
+            pltpu.SemaphoreType.DMA((5,)),
         ],
         compiler_params=pltpu.CompilerParams(vmem_limit_bytes=16 << 20),
         name="collide",
     )(*(pltpu.with_memory_space_constraint(a, pltpu.HBM) for a in (populations, cell_type, adjoint)))
-    xl = lax.ppermute(xp, axes, along(1, 0))
-    xr = lax.ppermute(xm, axes, along(-1, 0))
-    gu = lax.ppermute(gp, axes, across(1))
-    gd = lax.ppermute(gm, axes, across(-1))
-    top = jnp.concatenate([xl[rows - 1 : rows], xr[rows - 1 : rows]], axis=1)
-    bottom = jnp.concatenate([xl[0:1], xr[0:1]], axis=1)
-    yp = lax.dynamic_update_slice(yp, top, (CORNER_ROW, 0))
-    ym = lax.dynamic_update_slice(ym, bottom, (CORNER_ROW, 0))
-    yu = lax.ppermute(yp, axes, along(0, 1))
-    yd = lax.ppermute(ym, axes, along(0, -1))
-    flow_next, vel = pl.pallas_call(
+
+    def move(value, pairs):
+        return lax.ppermute(value, axes, pairs)
+
+    xa = move(xa, swaps(0, nx, 0))
+    xb = move(xb, swaps(0, nx, 1))
+    ga = move(ga, swaps(1, ny, 0))
+    gb = move(gb, swaps(1, ny, 1))
+    odd_x, odd_y = (lax.axis_index(axis) % 2 for axis in ("gx", "gz"))
+
+    def corners(row):
+        first, second = xa[row : row + 1], xb[row : row + 1]
+        return jnp.where(
+            odd_x == 0,
+            jnp.concatenate([second, first], axis=1),
+            jnp.concatenate([first, second], axis=1),
+        )
+
+    high, low = corners(rows - 1), corners(0)
+    ya = lax.dynamic_update_slice(ya, jnp.where(odd_y == 0, high, low), (CORNER_ROW, 0))
+    yb = lax.dynamic_update_slice(yb, jnp.where(odd_y == 0, low, high), (CORNER_ROW, 0))
+    ya = move(ya, swaps(3, ny * nz, 0))
+    yb = move(yb, swaps(3, ny * nz, 1))
+    planes = f32(3 * layers + 1, rows, cols)
+    flow_next, pa, pb, pc, own = pl.pallas_call(
         stream_kernel,
-        out_shape=(f32(*populations.shape), f32(nz, 3 * layers + 1, rows, cols)),
+        out_shape=(f32(*populations.shape), planes, planes, planes, planes),
         in_specs=[VMEM] * 8,
-        out_specs=(VMEM,) * 2,
-        scratch_shapes=[pltpu.VMEM((2, 8, LANES), jnp.float32)],
+        out_specs=(VMEM,) * 5,
+        scratch_shapes=[
+            pltpu.VMEM((2, 8, LANES), jnp.float32),
+            pltpu.VMEM((2, HEAT_ROW, cols), jnp.float32),
+            pltpu.VMEM((2, 3 * layers, rows, cols), jnp.float32),
+        ],
         compiler_params=pltpu.CompilerParams(vmem_limit_bytes=16 << 20),
         name="stream",
-    )(post, ysh, populations, cell_type, xl, xr, yu, yd)
-    va = lax.all_to_all(vel, "gz", split_axis=0, concat_axis=0, tiled=True)
+    )(post, ysh, populations, cell_type, xa, xb, ya, yb)
+    pa = move(pa, inside(((1, 2), (0, 3), (3, 0))))
+    pb = move(pb, inside(((0, 2), (1, 3))))
+    pc = move(pc, inside(((2, 3), (3, 2), (1, 0))))
     adjoint_prev = pl.pallas_call(
-        functools.partial(thermal_kernel, nz),
+        thermal_kernel,
         out_shape=f32(*adjoint.shape),
-        in_specs=[VMEM] * 8,
+        in_specs=[VMEM] * 11,
         out_specs=VMEM,
         scratch_shapes=[pltpu.VMEM((3 * layers + 1, heat_rows, cols), jnp.float32)],
         compiler_params=pltpu.CompilerParams(vmem_limit_bytes=16 << 20),
         name="thermal",
-    )(adjoint, va, xl, xr, yu, yd, gu, gd)
+    )(adjoint, pa, pb, pc, own, xa, xb, ya, yb, ga, gb)
     return flow_next, adjoint_prev
 
 

time: 46.4 us -> 50 us (1.078)
  the two profiles are of different devices: /device:TPU:243 before, /device:TPU:259 now
where the time goes in v1:
time: 50 us; the launch traced here: 49.6 us
  starting transfers between devices  32.5 us (65%)
  waiting for transfers between devices  12.1 us (24%)
  Pallas kernels  4.04 us (8%)
  between operations  0.82 us (2%)
    ppermute x9, starting transfers between devices, move(): return lax.ppermute(value, axes, pairs)  32.5 us
    ppermute x9, waiting for transfers between devices, move(): return lax.ppermute(value, axes, pairs)  12.1 us
    pallas_call x1, Pallas kernels, per_device(): pl.pallas_call(collide_kernel, out_shape=(f32(19, TOP, rows, cols), f32(1...  1.69 us
    pallas_call x1, Pallas kernels, per_device(): pl.pallas_call(stream_kernel, out_shape=(f32(*populations.shape), planes,...  1.4 us
  transfers between devices with their start and end apart: 9, of which 3 were waited for; matrix products, arithmetic and copies ran while one was open for 0% of the time, Pallas kernels for 0%

profile of v1, /device:TPU:259, one launch (start us, length us, event | category | flops | bytes accessed | tf_op | source)
XLA Modules:
  0.0 49.6 jit_solution(9918895840784185323)
XLA Ops:
  0.6 0.0 copy-start.2
  0.6 0.0 copy-start
  0.6 1.7 %collide.1 = (f32[19,8,4,256]{3,2,1,0:T(4,128)S(1)}, f32[10,8,4,256]{3,2,1,0:T(4,128)S(1)}, f32[16,128]{1,0:T(8,128)S(1)}, f32[16,128]{1,0:T(8,128)S(1)}, f32[64...) custom-call(f32[19,16,4,256]{3,2,1,0:T(4,128)} %pops.1, ...), custom_call_target="tpu_custom_call" | custom-call | tf_op jit(solution)/shard_map/collide/pallas_call | solution.py:360
  2.4 7.5 %collective-permute-start = (f32[16,128]{1,0:T(8,128)S(1)}, f32[16,128]{1,0:T(8,128)S(1)}, u32[]{:S(2)}, u32[]{:S(2)}) collective-permute-start(f32[16,128]{1,0:T(8,128)S(1)} %get-tuple-element.17), channel_id=1, source_target_pairs={{0,32},{1,33},{2,34},{3,35},{4,36},{5,37},{6,38},{7,39},{8,40},{9,... | collective-permute-start | bytes 24584 | tf_op jit(solution)/shard_map/ppermute | solution.py:386
  9.8 1.9 %collective-permute-start.1 = (f32[16,128]{1,0:T(8,128)S(1)}, f32[16,128]{1,0:T(8,128)S(1)}, u32[]{:S(2)}, u32[]{:S(2)}) collective-permute-start(f32[16,128]{1,0:T(8,128)S(1)} %get-tuple-element.18), channel_id=1, source_target_pairs={{32,64},{33,65},{34,66},{35,67},{36,68},{37,69},{38,70},{39,71},{4... | collective-permute-start | bytes 24584 | tf_op jit(solution)/shard_map/ppermute | solution.py:386
  11.7 0.0 copy-start.1
  11.8 0.0 collective-permute-done.xa
  11.8 8.4 %collective-permute-done.1.xb = f32[16,128]{1,0:T(8,128)S(1)} collective-permute-done((f32[16,128]{1,0:T(8,128)S(1)}, f32[16,128]{1,0:T(8,128)S(1)}, u32[]{:S(2)}, u32[]{:S(2)}) %collective-permute-start.1) | collective-permute-done | bytes 8224 | tf_op jit(solution)/shard_map/ppermute | solution.py:386
  20.3 2.2 %collective-permute-start.2 = (f32[64,256]{1,0:T(8,128)S(1)}, f32[64,256]{1,0:T(8,128)S(1)}, u32[]{:S(2)}, u32[]{:S(2)}) collective-permute-start(f32[64,256]{1,0:T(8,128)S(1)} %dynamic_update_slice.6), channel_id=1, source_target_pairs={{0,1},{1,0},{2,3},{3,2},{4,5},{5,4},{6,7},{7,6},{8,9},{9,8},{10,11... | collective-permute-start | bytes 196616 | tf_op jit(solution)/shard_map/ppermute | solution.py:386
  22.5 3.8 %collective-permute-start.3 = (f32[64,256]{1,0:T(8,128)S(1)}, f32[64,256]{1,0:T(8,128)S(1)}, u32[]{:S(2)}, u32[]{:S(2)}) collective-permute-start(f32[64,256]{1,0:T(8,128)S(1)} %dynamic_update_slice.7), channel_id=1, source_target_pairs={{1,2},{2,1},{3,4},{4,3},{5,6},{6,5},{7,8},{8,7},{9,10},{10,9},{11,... | collective-permute-start | bytes 196616 | tf_op jit(solution)/shard_map/ppermute | solution.py:386
  26.3 0.0 collective-permute-done.2.ya
  26.3 1.9 %collective-permute-done.3.yb = f32[64,256]{1,0:T(8,128)S(1)} collective-permute-done((f32[64,256]{1,0:T(8,128)S(1)}, f32[64,256]{1,0:T(8,128)S(1)}, u32[]{:S(2)}, u32[]{:S(2)}) %collective-permute-start.3) | collective-permute-done | bytes 65568 | tf_op jit(solution)/shard_map/ppermute | solution.py:386
  28.2 0.0 copy-done.2
  28.2 0.0 copy-done
  28.2 1.4 %stream.1 = (f32[19,16,4,256]{3,2,1,0:T(4,128)}, f32[13,4,256]{2,1,0:T(4,128)S(1)}, f32[13,4,256]{2,1,0:T(4,128)S(1)}, f32[13,4,256]{2,1,0:T(4,128)S(1)}, f32[13,4,256]{2,1,0:T(4,128)S(1)}) custom-call(f32[19,8,4,256]{3,2,1,0:T(4,128)S(1)} %get-tuple-element.15.post, f32[10,8,4,256]{3,2,1,0:T(4,128)S(1)} %get-tuple-element.16.ysh, ...), custom_call_target="tpu_custom_call" | custom-call | tf_op jit(solution)/shard_map/stream/pallas_call | solution.py:408
  29.6 3.1 %collective-permute-start.4 = (f32[13,4,256]{2,1,0:T(4,128)S(1)}, f32[13,4,256]{2,1,0:T(4,128)S(1)}, u32[]{:S(2)}, u32[]{:S(2)}) collective-permute-start(f32[13,4,256]{2,1,0:T(4,128)S(1)} %get-tuple-element.22), channel_id=1, source_target_pairs={{1,2},{0,3},{3,0},{5,6},{4,7},{7,4},{9,10},{8,11},{11,8},{13,14},{... | collective-permute-start | bytes 159752 | tf_op jit(solution)/shard_map/ppermute | solution.py:386
  32.7 6.0 %collective-permute-start.5 = (f32[13,4,256]{2,1,0:T(4,128)S(1)}, f32[13,4,256]{2,1,0:T(4,128)S(1)}, u32[]{:S(2)}, u32[]{:S(2)}) collective-permute-start(f32[13,4,256]{2,1,0:T(4,128)S(1)} %get-tuple-element.23), channel_id=1, source_target_pairs={{0,2},{1,3},{4,6},{5,7},{8,10},{9,11},{12,14},{13,15},{16,18},{17,... | collective-permute-start | bytes 159752 | tf_op jit(solution)/shard_map/ppermute | solution.py:386
  38.7 1.3 %collective-permute-start.6 = (f32[13,4,256]{2,1,0:T(4,128)S(1)}, f32[13,4,256]{2,1,0:T(4,128)S(1)}, u32[]{:S(2)}, u32[]{:S(2)}) collective-permute-start(f32[13,4,256]{2,1,0:T(4,128)S(1)} %get-tuple-element.24), channel_id=1, source_target_pairs={{2,3},{3,2},{1,0},{6,7},{7,6},{5,4},{10,11},{11,10},{9,8},{14,15},... | collective-permute-start | bytes 159752 | tf_op jit(solution)/shard_map/ppermute | solution.py:386
  40.0 3.7 %collective-permute-start.7 = (f32[4,256]{1,0:T(4,128)S(1)}, f32[4,256]{1,0:T(4,128)S(1)}, u32[]{:S(2)}, u32[]{:S(2)}) collective-permute-start(f32[4,256]{1,0:T(4,128)S(1)} %get-tuple-element.26), channel_id=1, source_target_pairs={{0,4},{1,5},{2,6},{3,7},{4,0},{5,1},{6,2},{7,3},{8,12},{9,13},{10,... | collective-permute-start | bytes 12296 | tf_op jit(solution)/shard_map/ppermute | solution.py:386
  43.7 3.1 %collective-permute-start.8 = (f32[4,256]{1,0:T(4,128)S(1)}, f32[4,256]{1,0:T(4,128)S(1)}, u32[]{:S(2)}, u32[]{:S(2)}) collective-permute-start(f32[4,256]{1,0:T(4,128)S(1)} %get-tuple-element.27), channel_id=1, source_target_pairs={{4,8},{5,9},{6,10},{7,11},{8,4},{9,5},{10,6},{11,7},{12,16},{13,17... | collective-permute-start | bytes 12296 | tf_op jit(solution)/shard_map/ppermute | solution.py:386
  46.8 0.0 collective-permute-done.7.ga
  46.8 1.8 %collective-permute-done.8.gb = f32[4,256]{1,0:T(4,128)S(1)} collective-permute-done((f32[4,256]{1,0:T(4,128)S(1)}, f32[4,256]{1,0:T(4,128)S(1)}, u32[]{:S(2)}, u32[]{:S(2)}) %collective-permute-start.8) | collective-permute-done | bytes 4128 | tf_op jit(solution)/shard_map/ppermute | solution.py:386
  48.6 0.0 collective-permute-done.4.pa
  48.6 0.0 collective-permute-done.5.pb
  48.7 0.0 collective-permute-done.6.pc
  48.7 0.0 copy-done.1
  48.7 0.9 %thermal.1 = f32[7,4,16,256]{3,2,1,0:T(8,128)} custom-call(f32[7,4,16,256]{3,2,1,0:T(8,128)S(1)} %copy-done.1, f32[13,4,256]{2,1,0:T(4,128)S(1)} %collective-permute-done.4.pa, f32[13,4,256]{2,1,0:T(4,128)S(1)} %collective-permute-done.5.pb, f32[13,4,256]{2,1,0:T(4,128)S(1)} %collective-permute-done.6.pc, f32[13,4,256]{2,1,0:T(4,128)S(1)} %get-tuple-element.25.own, ...), custom_call_target="tpu_custom_call" | custom-call | tf_op jit(solution)/shard_map/thermal/pallas_call | solution.py:424
  (6 shorter events, 0.1 us)
Async XLA Ops:
  0.6 27.5 %copy-start.2 = (s32[16,4,256]{2,1,0:T(4,128)S(1)}, s32[16,4,256]{2,1,0:T(4,128)}, u32[]{:S(2)}) copy-start(s32[16,4,256]{2,1,0:T(4,128)} %cells.1) | copy-start | bytes 196612
  0.6 27.5 %copy-start = (f32[19,16,4,256]{3,2,1,0:T(4,128)S(1)}, f32[19,16,4,256]{3,2,1,0:T(4,128)}, u32[]{:S(2)}) copy-start(f32[19,16,4,256]{3,2,1,0:T(4,128)} %pops.1) | copy-start | bytes 3735556
  2.4 9.4 %collective-permute-start = (f32[16,128]{1,0:T(8,128)S(1)}, f32[16,128]{1,0:T(8,128)S(1)}, u32[]{:S(2)}, u32[]{:S(2)}) collective-permute-start(f32[16,128]{1,0:T(8,128)S(1)} %get-tuple-element.17), channel_id=1, source_target_pairs={{0,32},{1,33},{2,34},{3,35},{4,36},{5,37},{6,38},{7,39},{8,40},{9,... | collective-permute-start | bytes 24584 | tf_op jit(solution)/shard_map/ppermute | solution.py:386
  9.8 10.4 %collective-permute-start.1 = (f32[16,128]{1,0:T(8,128)S(1)}, f32[16,128]{1,0:T(8,128)S(1)}, u32[]{:S(2)}, u32[]{:S(2)}) collective-permute-start(f32[16,128]{1,0:T(8,128)S(1)} %get-tuple-element.18), channel_id=1, source_target_pairs={{32,64},{33,65},{34,66},{35,67},{36,68},{37,69},{38,70},{39,71},{4... | collective-permute-start | bytes 24584 | tf_op jit(solution)/shard_map/ppermute | solution.py:386
  11.7 36.9 %copy-start.1 = (f32[7,4,16,256]{3,2,1,0:T(8,128)S(1)}, f32[7,4,16,256]{3,2,1,0:T(8,128)}, u32[]{:S(2)}) copy-start(f32[7,4,16,256]{3,2,1,0:T(8,128)} %adj.1) | copy-start | bytes 1376260
  20.3 6.0 %collective-permute-start.2 = (f32[64,256]{1,0:T(8,128)S(1)}, f32[64,256]{1,0:T(8,128)S(1)}, u32[]{:S(2)}, u32[]{:S(2)}) collective-permute-start(f32[64,256]{1,0:T(8,128)S(1)} %dynamic_update_slice.6), channel_id=1, source_target_pairs={{0,1},{1,0},{2,3},{3,2},{4,5},{5,4},{6,7},{7,6},{8,9},{9,8},{10,11... | collective-permute-start | bytes 196616 | tf_op jit(solution)/shard_map/ppermute | solution.py:386
  22.5 5.7 %collective-permute-start.3 = (f32[64,256]{1,0:T(8,128)S(1)}, f32[64,256]{1,0:T(8,128)S(1)}, u32[]{:S(2)}, u32[]{:S(2)}) collective-permute-start(f32[64,256]{1,0:T(8,128)S(1)} %dynamic_update_slice.7), channel_id=1, source_target_pairs={{1,2},{2,1},{3,4},{4,3},{5,6},{6,5},{7,8},{8,7},{9,10},{10,9},{11,... | collective-permute-start | bytes 196616 | tf_op jit(solution)/shard_map/ppermute | solution.py:386
  29.6 19.1 %collective-permute-start.4 = (f32[13,4,256]{2,1,0:T(4,128)S(1)}, f32[13,4,256]{2,1,0:T(4,128)S(1)}, u32[]{:S(2)}, u32[]{:S(2)}) collective-permute-start(f32[13,4,256]{2,1,0:T(4,128)S(1)} %get-tuple-element.22), channel_id=1, source_target_pairs={{1,2},{0,3},{3,0},{5,6},{4,7},{7,4},{9,10},{8,11},{11,8},{13,14},{... | collective-permute-start | bytes 159752 | tf_op jit(solution)/shard_map/ppermute | solution.py:386
  32.7 15.9 %collective-permute-start.5 = (f32[13,4,256]{2,1,0:T(4,128)S(1)}, f32[13,4,256]{2,1,0:T(4,128)S(1)}, u32[]{:S(2)}, u32[]{:S(2)}) collective-permute-start(f32[13,4,256]{2,1,0:T(4,128)S(1)} %get-tuple-element.23), channel_id=1, source_target_pairs={{0,2},{1,3},{4,6},{5,7},{8,10},{9,11},{12,14},{13,15},{16,18},{17,... | collective-permute-start | bytes 159752 | tf_op jit(solution)/shard_map/ppermute | solution.py:386
  38.7 10.0 %collective-permute-start.6 = (f32[13,4,256]{2,1,0:T(4,128)S(1)}, f32[13,4,256]{2,1,0:T(4,128)S(1)}, u32[]{:S(2)}, u32[]{:S(2)}) collective-permute-start(f32[13,4,256]{2,1,0:T(4,128)S(1)} %get-tuple-element.24), channel_id=1, source_target_pairs={{2,3},{3,2},{1,0},{6,7},{7,6},{5,4},{10,11},{11,10},{9,8},{14,15},... | collective-permute-start | bytes 159752 | tf_op jit(solution)/shard_map/ppermute | solution.py:386
  40.0 6.8 %collective-permute-start.7 = (f32[4,256]{1,0:T(4,128)S(1)}, f32[4,256]{1,0:T(4,128)S(1)}, u32[]{:S(2)}, u32[]{:S(2)}) collective-permute-start(f32[4,256]{1,0:T(4,128)S(1)} %get-tuple-element.26), channel_id=1, source_target_pairs={{0,4},{1,5},{2,6},{3,7},{4,0},{5,1},{6,2},{7,3},{8,12},{9,13},{10,... | collective-permute-start | bytes 12296 | tf_op jit(solution)/shard_map/ppermute | solution.py:386
  43.7 4.9 %collective-permute-start.8 = (f32[4,256]{1,0:T(4,128)S(1)}, f32[4,256]{1,0:T(4,128)S(1)}, u32[]{:S(2)}, u32[]{:S(2)}) collective-permute-start(f32[4,256]{1,0:T(4,128)S(1)} %get-tuple-element.27), channel_id=1, source_target_pairs={{4,8},{5,9},{6,10},{7,11},{8,4},{9,5},{10,6},{11,7},{12,16},{13,17... | collective-permute-start | bytes 12296 | tf_op jit(solution)/shard_map/ppermute | solution.py:386
